TPU v7x, 32 devices: a whole 2x2x4 slice. The times are simulated.
32 devices in a mesh: rep: 8 (over z, core), rows: 4 (over y, x).
Axes of the slice: x: 2, y: 2, z: 4, core: 2. Of those that a mesh axis runs over, the one named last changes fastest.
Arguments:
- weights: bfloat16 [7168, 2048], P('rows'), may hold values from -6 to 6
- momentum: float32 [8, 7168, 2048], P('rep', 'rows'), may hold values from -8 to 8
- gradient: bfloat16 [8, 7168, 2048], P('rep', 'rows'), may hold values from -8 to 8
- right_factor: float32 [2048, 512], P('rows'), may hold values from -6 to 6
Outputs:
- new_weights: bfloat16 [7168, 2048], P('rows')
- new_momentum: float32 [8, 7168, 2048], P('rep', 'rows')
- new_right: float32 [2048, 512], P('rows')
All inputs are finite; a program needn't handle non-finite values.
Results may differ from a plain program's by a relative error of at most 0.019.
Values may be sent and summed in bfloat16 or wider, within the bound.
A program may use at most 128 MiB of HBM per device.

v0:
```python
import jax
import jax.numpy as jnp
from jax import lax
from jax.sharding import PartitionSpec as P

M = 7168
N = 2048


momentum_keep = 0.05
learn_rate = 0.5
tiny = 1e-06


def per_device(weights, momentum, gradient, right_factor):
    groups = lax.axis_size("rep")
    shards = lax.axis_size("rows")
    combined = momentum[0] + gradient[0].astype(jnp.float32)
    combined_half = combined.astype(jnp.bfloat16)
    columns = combined.shape[1]
    share = columns // shards
    left_local = jnp.dot(
        combined_half,
        lax.all_gather(right_factor.astype(jnp.bfloat16), "rows", axis=0, tiled=True),
        preferred_element_type=jnp.float32,
    )
    left_local = lax.optimization_barrier(left_local.astype(jnp.bfloat16)).astype(jnp.float32)
    left_mean = lax.psum(left_local.astype(jnp.bfloat16), "rep").astype(jnp.float32) / groups
    gram = lax.psum(jnp.dot(left_mean.T, left_mean, precision=lax.Precision.HIGHEST), "rows")
    chol = jnp.linalg.cholesky(gram)
    left_orth = jax.scipy.linalg.solve_triangular(chol, left_mean.T, lower=True).T
    left_half = left_orth.astype(jnp.bfloat16)
    partial_right = jnp.einsum(
        "ij,ik->jk", combined_half, left_half, preferred_element_type=jnp.float32
    )
    right_mean = lax.psum(partial_right, ("rep", "rows")) / groups
    normed = right_mean / jnp.sqrt(jnp.mean(right_mean * right_mean, axis=0) + tiny)
    feedback = jnp.dot(
        left_half, right_mean.astype(jnp.bfloat16).T, preferred_element_type=jnp.float32
    )
    update = jnp.dot(left_half, normed.astype(jnp.bfloat16).T, preferred_element_type=jnp.float32)
    new_right = lax.dynamic_slice_in_dim(normed, lax.axis_index("rows") * share, share, 0)
    new_momentum = combined - momentum_keep * feedback
    new_weights = (weights.astype(jnp.float32) - learn_rate * jnp.sqrt(M / N) * update).astype(
        jnp.bfloat16
    )
    return (new_weights, new_momentum[None], new_right)


def solution(mesh):
    in_specs = (P("rows", None), P("rep", "rows", None), P("rep", "rows", None), P("rows", None))
    out_specs = (P("rows", None), P("rep", "rows", None), P("rows", None))
    return jax.shard_map(
        per_device, mesh=mesh, in_specs=in_specs, out_specs=out_specs, check_vma=False
    )
```

profile of v0, /device:TPU:0, one launch (start us, length us, event | category | flops | bytes accessed | tf_op | source)
XLA Modules:
  0.0 525.9 jit_solution(10342217912073874617)
XLA Ops:
  7.2 2.1 convert_element_type.35
  9.4 39.0 %all-gather.2.cloned.1.call-done = bf16[2048,512]{1,0:T(8,128)(2,1)} async-done(((bf16[512,512]{1,0:T(8,128)(2,1)}), bf16[2048,512]{1,0:T(8,128)(2,1)}) %all-gather.2.cloned.1.call-update) | async-done | bytes 2097168 | tf_op jit(solution)/shard_map/all_gather | solution.py:24
  48.3 13.1 %convolution_convert_fusion = bf16[1792,512]{1,0:T(8,128)(2,1)} fusion(bf16[2048,512]{1,0:T(8,128)(2,1)} %all-gather.2.cloned.1.call-done, f32[1,1792,2048]{2,1,0:T(8,128)} %param.5, bf16[1,1792,2048]{2,1,0:T(8,128)(2,1)} %param.6), kind=kOutput, calls=%fused_computation.13 | convolution fusion | flops 3770023936 | bytes 25952256 | tf_op jit(solution)/shard_map/dot_general | solution.py:22
  61.5 63.3 %all-reduce.5.cloned.1.call-done = bf16[1792,512]{1,0:T(8,128)(2,1)} async-done(((bf16[1792,512]{1,0:T(8,128)(2,1)}), bf16[1792,512]{1,0:T(8,128)(2,1)}) %all-reduce.5.cloned.1.call-update) | async-done | bytes 1835024 | tf_op jit(solution)/shard_map/psum | solution.py:28
  124.7 9.4 %fusion.2 = f32[512,512]{0,1:T(8,128)} fusion(bf16[1792,512]{1,0:T(8,128)(2,1)} %all-reduce.5.cloned.1.call-done), kind=kOutput, calls=%fused_computation.12 | convolution fusion | flops 5638979584 | bytes 2883584 | tf_op jit(solution)/shard_map/dot_general | solution.py:29
  134.4 2.4 fusion.1
  136.8 50.0 %all-reduce.7.cloned.1.call-done = f32[512,512]{0,1:T(8,128)} async-done(((f32[512,512]{0,1:T(8,128)}), f32[512,512]{0,1:T(8,128)}) %all-reduce.7.cloned.1.call-update) | async-done | bytes 1048592 | tf_op jit(solution)/shard_map/psum | solution.py:29
  186.8 1.6 copy.8
  188.3 1.4 fusion.18
  189.8 11.7 %cholesky.104 = f32[128,128]{1,0:T(8,128)S(1)} custom-call(f32[128,128]{1,0:T(8,128)S(1)} %cholesky.266), custom_call_target="Cholesky" | custom-call | tf_op jit(solution)/shard_map/jit(cholesky)/cholesky | solution.py:30
  201.5 9.8 %custom-call.31 = f32[1,128,128]{1,2,0:T(8,128)S(1)} custom-call(f32[1,128,128]{2,1,0:T(8,128)S(1)} %get-tuple-element.30), custom_call_target="InvertDiagBlocksLowerTriangular" | custom-call | tf_op jit(solution)/shard_map/jit(cholesky)/cholesky | solution.py:30
  212.2 11.7 %cholesky.217 = f32[128,128]{1,0:T(8,128)S(1)} custom-call(f32[128,128]{1,0:T(8,128)S(1)} %cholesky.270), custom_call_target="Cholesky" | custom-call | tf_op jit(solution)/shard_map/jit(cholesky)/cholesky | solution.py:30
  223.9 10.2 %custom-call.32 = f32[1,128,128]{1,2,0:T(8,128)S(1)} custom-call(f32[1,128,128]{2,1,0:T(8,128)S(1)} %get-tuple-element.27), custom_call_target="InvertDiagBlocksLowerTriangular" | custom-call | tf_op jit(solution)/shard_map/jit(cholesky)/cholesky | solution.py:30
  234.8 11.7 %cholesky.238 = f32[128,128]{1,0:T(8,128)S(1)} custom-call(f32[128,128]{1,0:T(8,128)S(1)} %cholesky.275), custom_call_target="Cholesky" | custom-call | tf_op jit(solution)/shard_map/jit(cholesky)/cholesky | solution.py:30
  247.3 9.8 %custom-call.33 = f32[1,128,128]{1,2,0:T(8,128)S(1)} custom-call(f32[1,128,128]{2,1,0:T(8,128)S(1)} %get-tuple-element.24), custom_call_target="InvertDiagBlocksLowerTriangular" | custom-call | tf_op jit(solution)/shard_map/jit(cholesky)/cholesky | solution.py:30
  257.7 11.9 %cholesky.255 = f32[128,128]{1,0:T(8,128)S(1)} custom-call(f32[128,128]{1,0:T(8,128)S(1)} %convolution_subtract_fusion.4), custom_call_target="Cholesky" | custom-call | tf_op jit(solution)/shard_map/jit(cholesky)/cholesky | solution.py:30
  273.6 8.5 %while.1 = (s32[]{:T(128)}, f32[512,512]{1,0:T(8,128)S(1)}, s32[4,2]{0,1:T(2,128)S(1)}, f32[4,128,128]{2,1,0:T(8,128)S(1)}, s32[]{:T(128)}) while((s32[]{:T(128)}, f32[512,512]{1,0:T(8,128)S(1)}, s32[4,2]{0,1:T(2,128)S(1)}, f32[4,128,128]{2,1,0:T(8,128)S(1)}, s32[]{:T(128)}) %tuple.34), condition=%wide.while_cond, body=%wide.while_body.sunk | while | flops 2 | bytes 131181 | solution.py:31
  274.3 1.4 bitcast_dynamic-update-slice_fusion.2
  276.4 1.4 bitcast_dynamic-update-slice_fusion.2
  278.5 1.4 bitcast_dynamic-update-slice_fusion.2
  280.6 1.4 bitcast_dynamic-update-slice_fusion.2
  282.1 39.3 %custom-call.34 = f32[4,128,128]{1,2,0:T(8,128)S(1)} custom-call(f32[4,128,128]{2,1,0:T(8,128)S(1)} %get-tuple-element.10), custom_call_target="InvertDiagBlocksLowerTriangular" | custom-call | tf_op jit(solution)/shard_map/jit(_solve_triangular)/triangular_solve | solution.py:31
  321.4 2.3 fusion.45
  323.7 2.8 convolution_subtract_fusion.1
  327.5 3.2 convolution_subtract_fusion
  331.7 4.7 fusion.9
  336.3 1.2 convolution_convert_fusion.1
  338.3 11.3 %fusion.41 = f32[2048,512]{1,0:T(8,128)} fusion(f32[1,1792,2048]{2,1,0:T(8,128)} %param.5, bf16[1,1792,2048]{2,1,0:T(8,128)(2,1)S(1)} %bitcast.67, bf16[128,1792]{1,0:T(8,128)(2,1)S(1)} %convolution_convert_fusion.1, bf16[128,1792]{1,0:T(8,128)(2,1)S(1)} %get-tuple-element.33, bf16[128,1792]{1,0:T(8,128)(2,1)S(1)} %get-tuple-element.35, ...), kind=kOutput, calls=%fused_computation.86 | convolution fusion | flops 3776446464 | bytes 28049408 | tf_op jit(solution)/shard_map/ij,ik->jk/dot_general | solution.py:33
  349.6 142.5 %all-reduce.9.cloned.1.call-done = f32[2048,512]{1,0:T(8,128)} async-done(((f32[2048,512]{1,0:T(8,128)}), f32[2048,512]{1,0:T(8,128)}) %all-reduce.9.cloned.1.call-update) | async-done | bytes 4194320 | tf_op jit(solution)/shard_map/psum | solution.py:36
  492.1 2.9 multiply_reduce_fusion
  496.7 8.2 %subtract_convert_fusion = bf16[1792,2048]{1,0:T(8,128)(2,1)} fusion(bf16[1792,2048]{1,0:T(8,128)(2,1)} %param.4, f32[2048,512]{1,0:T(8,128)S(1)} %multiply_divide_fusion, bf16[128,1792]{1,0:T(8,128)(2,1)S(1)} %copy-done.6, bf16[128,1792]{1,0:T(8,128)(2,1)S(1)} %copy-done.4, bf16[128,1792]{1,0:T(8,128)(2,1)S(1)} %get-tuple-element.35, ...), kind=kOutput, calls=%fused_computation.5 | convolution fusion | flops 3781165056 | bytes 20709376 | tf_op jit(solution)/shard_map/dot_general | solution.py:41
  506.0 13.0 %fusion = f32[1,1792,2048]{2,1,0:T(8,128)} fusion(f32[1,1792,2048]{2,1,0:T(8,128)} %param.5, bf16[1,1792,2048]{2,1,0:T(8,128)(2,1)} %param.6, f32[2048,512]{1,0:T(8,128)S(1)} %copy-done, bf16[128,1792]{1,0:T(8,128)(2,1)} %copy-done.5, bf16[128,1792]{1,0:T(8,128)(2,1)} %copy-done.3, bf16[128,1792]{1,0:T(8,128)(2,1)S(1)} %get-tuple-element.35, ...), kind=kOutput, calls=%fused_computation.4 | convolution fusion | flops 3782213632 | bytes 42729472 | tf_op jit(solution)/shard_map/dot_general | solution.py:38
  (61 shorter events, 12.9 us)
Async XLA Ops:
  7.2 41.2 %all-gather.2.cloned.1.call-start = ((), (), s32[]{:S(2)}) async-start(), calls=%async_computation | async-start | bytes 2621440 | tf_op jit(solution)/shard_map/all_gather | solution.py:24
  9.3 115.4 %all-reduce.5.cloned.1.call-start = ((), (), s32[]{:S(2)}) async-start(), calls=%async_computation.1 | async-start | bytes 3670016 | tf_op jit(solution)/shard_map/psum | solution.py:28
  61.4 125.4 %all-reduce.7.cloned.1.call-start = ((), (), s32[]{:S(2)}) async-start(), calls=%async_computation.2 | async-start | bytes 2097152 | tf_op jit(solution)/shard_map/psum | solution.py:29
  124.7 9.7 %copy-start.2 = (bf16[1792,512]{1,0:T(8,128)(2,1)S(1)}, bf16[1792,512]{1,0:T(8,128)(2,1)}, u32[]{:S(2)}) copy-start(bf16[1792,512]{1,0:T(8,128)(2,1)} %all-reduce.5.cloned.1.call-done) | copy-start | bytes 5505028
  134.1 358.0 %all-reduce.9.cloned.1.call-start = ((), (), s32[]{:S(2)}) async-start(), calls=%async_computation.3 | async-start | bytes 8388608 | tf_op jit(solution)/shard_map/psum | solution.py:36
  321.4 6.1 %copy-start.1 = (f32[512,1792]{0,1:T(8,128)S(1)}, f32[512,1792]{0,1:T(8,128)}, u32[]{:S(2)}) copy-start(f32[512,1792]{0,1:T(8,128)} %fusion.1) | copy-start | bytes 11010052
  326.5 11.8 %slice-start = ((s8[7340032]{0:T(1024)(128)(4,1)}), s8[4194304]{0:T(1024)(128)(4,1)S(1)}, s32[]{:S(2)}) async-start(s8[7340032]{0:T(1024)(128)(4,1)} %bitcast.66), calls=%async_computation.4 | async-start | bytes 8388608
  330.7 7.6 %slice-start.1 = ((s8[7340032]{0:T(1024)(128)(4,1)}), s8[3145728]{0:T(1024)(128)(4,1)S(1)}, s32[]{:S(2)}) async-start(s8[7340032]{0:T(1024)(128)(4,1)} %bitcast.66), calls=%async_computation.5 | async-start | bytes 6291456
  331.7 17.9 %copy-start.3 = (bf16[128,1792]{1,0:T(8,128)(2,1)}, bf16[128,1792]{1,0:T(8,128)(2,1)S(1)}, u32[]{:S(2)}) copy-start(bf16[128,1792]{1,0:T(8,128)(2,1)S(1)} %get-tuple-element.33) | copy-start | bytes 1376260
  337.5 0.8 copy-start.5
  492.1 3.4 copy-start
  495.6 1.0 copy-start.4
  495.6 1.2 copy-start.6
Sparse Core Ops, SparseCore 0:
  10.4 37.8 all-gather.1
  61.5 63.1 all-reduce.4
  134.3 52.4 all-reduce.6
  349.7 142.3 all-reduce.8
where the time goes:
time: 534 us; the launch traced here: 526 us
  waiting for transfers between devices  295 us (55%)
  other arithmetic  128 us (24%)
  matrix products  72.8 us (14%)
  between operations  17 us (3%)
  local copies, waits for them, and re-layouts  13.1 us (2%)
    psum x1, waiting for transfers between devices, per_device(): right_mean = lax.psum(partial_right, ('rep', 'rows')) / groups  143 us
    another operation x14, other arithmetic, per_device(): chol = jnp.linalg.cholesky(gram)  79 us
    psum x1, waiting for transfers between devices, per_device(): lax.psum(left_local.astype(jnp.bfloat16), 'rep').astype(jnp.float32)  63.3 us
    psum x1, waiting for transfers between devices, per_device(): lax.psum(jnp.dot(left_mean.T, left_mean, precision=lax.Precision.HIGHEST)...  50 us
    another operation x3, other arithmetic, per_device(): jax.scipy.linalg.solve_triangular(chol, left_mean.T, lower=True)  39.4 us
    all_gather x1, waiting for transfers between devices, per_device(): lax.all_gather(right_factor.astype(jnp.bfloat16), 'rows', axis=0, tiled=T...  39 us
    another operation x7, matrix products, per_device(): jax.scipy.linalg.solve_triangular(chol, left_mean.T, lower=True)  16 us
    dot_general x1, matrix products, per_device(): jnp.dot(combined_half, lax.all_gather(right_factor.astype(jnp.bfloat16),...  13.1 us
  transfers between devices with their start and end apart: 4, of which 4 were waited for; matrix products, arithmetic and copies ran while one was open for 0% of the time, Pallas kernels for 0%

commit v1 on v0

--- a/solution.py
+++ b/solution.py
@@ -1,6 +1,7 @@
-import jax
-import jax.numpy as jnp
+import jax, jax.numpy as jnp
 from jax import lax
+from jax.experimental import pallas as pl
+from jax.experimental.pallas import tpu as pltpu
 from jax.sharding import PartitionSpec as P
 
 M = 7168
@@ -10,6 +11,73 @@
 momentum_keep = 0.05
 learn_rate = 0.5
 tiny = 1e-06
+
+
+HI = lax.Precision.HIGHEST
+F32 = jnp.float32
+
+def dot_tn(a, b):
+    return lax.dot_general(a, b, (((0,), (0,)), ((), ())), precision=HI, preferred_element_type=F32)
+
+def factor_block(work, size, step):
+    wide = 2 * size
+    for at in range(0, size, step):
+        panel = work[at:at + step, :]
+        el = {}
+        for i in range(step):
+            for k in range(i + 1):
+                el[i, k] = jnp.broadcast_to(panel[k:k + 1, at + i:at + i + 1], (1, size))
+        rows = [(panel[i:i + 1, :size], panel[i:i + 1, size:]) for i in range(step)]
+        done = []
+        for k in range(step):
+            inv = lax.rsqrt(el[k, k])
+            own = (rows[k][0] * inv, rows[k][1] * inv)
+            done.append(own)
+            col = {i: el[i, k] * inv for i in range(k + 1, step)}
+            for i in range(k + 1, step):
+                rows[i] = (rows[i][0] - col[i] * own[0], rows[i][1] - col[i] * own[1])
+                for m in range(k + 1, i + 1):
+                    el[i, m] = el[i, m] - col[i] * col[m]
+        upper = jnp.concatenate([d[0] for d in done], axis=0)
+        aug = jnp.concatenate([d[1] for d in done], axis=0)
+        work[at:at + step, :size] = upper
+        work[at:at + step, size:] = aug
+        nxt = at + step
+        if nxt < size:
+            upd = dot_tn(upper, jnp.concatenate([upper, aug], axis=1))
+            work[nxt:, :] = work[nxt:, :] - upd[nxt:, :]
+
+def chol_kernel(size, step, gram_ref, out_ref, full, work):
+    rank = gram_ref.shape[0]
+    full[:, :rank] = gram_ref[...]
+    r = lax.broadcasted_iota(jnp.int32, (rank, rank), 0)
+    c = lax.broadcasted_iota(jnp.int32, (rank, rank), 1)
+    full[:, rank:] = jnp.where(r == c, 1.0, 0.0).astype(F32)
+    rb = lax.broadcasted_iota(jnp.int32, (size, size), 0)
+    cb = lax.broadcasted_iota(jnp.int32, (size, size), 1)
+    eye = jnp.where(rb == cb, 1.0, 0.0).astype(F32)
+    for at in range(0, rank, size):
+        work[:, :size] = full[at:at + size, at:at + size]
+        work[:, size:] = eye
+        factor_block(work, size, step)
+        inv = jnp.where(rb >= cb, work[:, size:], 0.0)
+        block = jnp.dot(inv, full[at:at + size, :], precision=HI, preferred_element_type=F32)
+        out_ref[at:at + size, :] = block[:, rank:]
+        nxt = at + size
+        if nxt < rank:
+            full[nxt:, :] = full[nxt:, :] - dot_tn(block[:, nxt:rank], block)
+
+def inverse_factor(gram):
+    rank = gram.shape[0]
+    size = 128
+    return pl.pallas_call(
+        lambda *refs: chol_kernel(size, 8, *refs),
+        out_shape=jax.ShapeDtypeStruct((rank, rank), F32),
+        in_specs=[pl.BlockSpec(memory_space=pltpu.VMEM)],
+        out_specs=pl.BlockSpec(memory_space=pltpu.VMEM),
+        scratch_shapes=[pltpu.VMEM((rank, 2 * rank), F32), pltpu.VMEM((size, 2 * size), F32)],
+        name="inverse_factor",
+    )(gram)
 
 
 def per_device(weights, momentum, gradient, right_factor):
@@ -27,8 +95,8 @@
     left_local = lax.optimization_barrier(left_local.astype(jnp.bfloat16)).astype(jnp.float32)
     left_mean = lax.psum(left_local.astype(jnp.bfloat16), "rep").astype(jnp.float32) / groups
     gram = lax.psum(jnp.dot(left_mean.T, left_mean, precision=lax.Precision.HIGHEST), "rows")
-    chol = jnp.linalg.cholesky(gram)
-    left_orth = jax.scipy.linalg.solve_triangular(chol, left_mean.T, lower=True).T
+    inverse = inverse_factor(gram)
+    left_orth = jnp.dot(left_mean, inverse.T, precision=lax.Precision.HIGHEST)
     left_half = left_orth.astype(jnp.bfloat16)
     partial_right = jnp.einsum(
         "ij,ik->jk", combined_half, left_half, preferred_element_type=jnp.float32

time: 534 us -> 430 us (0.81)
  other arithmetic: 128 us -> 5.48 us
  Pallas kernels: 0 us -> 37.8 us
  local copies, waits for them, and re-layouts: 13.1 us -> 1.63 us
  matrix products: 72.8 us -> 65.6 us
    another operation x17 -> x0, other arithmetic: 118 us -> none  [the longest x14 79 us: per_device(): chol = jnp.linalg.cholesky(gram)]
    pallas_call x0 -> x1, Pallas kernels: none -> 37.8 us  [inverse_factor(): pl.pallas_call(lambda *refs: chol_kernel(size, 8, *refs), out_shape=jax.S...]
    another operation x13 -> x0, matrix products: 17.9 us -> none  [the longest x7 16 us: per_device(): jax.scipy.linalg.solve_triangular(chol, left_mean.T, lower=True)]
    another operation x17 -> x0, local copies, waits for them, and re-layouts: 8.54 us -> none
    dot_general x0 -> x1, matrix products: none -> 7.94 us  [per_device(): left_orth = jnp.dot(left_mean, inverse.T, precision=lax.Precision.HIGHEST)]
where the time goes in v1:
time: 430 us; the launch traced here: 422 us
  waiting for transfers between devices  297 us (69%)
  matrix products  65.6 us (15%)
  Pallas kernels  37.8 us (9%)
  between operations  14.2 us (3%)
  other arithmetic  5.48 us (1%)
    psum x1, waiting for transfers between devices, per_device(): right_mean = lax.psum(partial_right, ('rep', 'rows')) / groups  142 us
    psum x1, waiting for transfers between devices, per_device(): lax.psum(left_local.astype(jnp.bfloat16), 'rep').astype(jnp.float32)  63.3 us
    psum x1, waiting for transfers between devices, per_device(): lax.psum(jnp.dot(left_mean.T, left_mean, precision=lax.Precision.HIGHEST)...  52.4 us
    all_gather x1, waiting for transfers between devices, per_device(): lax.all_gather(right_factor.astype(jnp.bfloat16), 'rows', axis=0, tiled=T...  39 us
    pallas_call x1, Pallas kernels, inverse_factor(): pl.pallas_call(lambda *refs: chol_kernel(size, 8, *refs), out_shape=jax.S...  37.8 us
    dot_general x1, matrix products, per_device(): jnp.einsum('ij,ik->jk', combined_half, left_half, preferred_element_type=...  14.4 us
    dot_general x1, matrix products, per_device(): jnp.dot(combined_half, lax.all_gather(right_factor.astype(jnp.bfloat16),...  13.1 us
    dot_general x1, matrix products, per_device(): jnp.dot(left_half, right_mean.astype(jnp.bfloat16).T, preferred_element_t...  12.6 us
  transfers between devices with their start and end apart: 4, of which 4 were waited for; matrix products, arithmetic and copies ran while one was open for 0% of the time, Pallas kernels for 0%

profile of v1, /device:TPU:0, one launch (start us, length us, event | category | flops | bytes accessed | tf_op | source)
XLA Modules:
  0.0 422.1 jit_solution(5973371746484589960)
XLA Ops:
  7.2 0.0 all-gather.2.cloned.1.call-start
  7.2 2.1 convert_element_type.36
  9.3 0.0 all-gather.2.cloned.1.call-update
  9.3 0.0 all-reduce.4.cloned.1.call-start
  9.4 39.0 %all-gather.2.cloned.1.call-done = bf16[2048,512]{1,0:T(8,128)(2,1)} async-done(((bf16[512,512]{1,0:T(8,128)(2,1)}), bf16[2048,512]{1,0:T(8,128)(2,1)}) %all-gather.2.cloned.1.call-update) | async-done | bytes 2097168 | tf_op jit(solution)/shard_map/all_gather | solution.py:92
  48.3 13.1 %convolution_convert_fusion = bf16[1792,512]{1,0:T(8,128)(2,1)} fusion(bf16[2048,512]{1,0:T(8,128)(2,1)} %all-gather.2.cloned.1.call-done, f32[1,1792,2048]{2,1,0:T(8,128)} %param.5, bf16[1,1792,2048]{2,1,0:T(8,128)(2,1)} %param.6), kind=kOutput, calls=%fused_computation.12 | convolution fusion | flops 3770023936 | bytes 25952256 | tf_op jit(solution)/shard_map/dot_general | solution.py:90
  61.4 0.0 all-reduce.4.cloned.1.call-update
  61.4 0.0 all-reduce.6.cloned.1.call-start
  61.5 63.3 %all-reduce.4.cloned.1.call-done = bf16[1792,512]{1,0:T(8,128)(2,1)} async-done(((bf16[1792,512]{1,0:T(8,128)(2,1)}), bf16[1792,512]{1,0:T(8,128)(2,1)}) %all-reduce.4.cloned.1.call-update) | async-done | bytes 1835024 | tf_op jit(solution)/shard_map/psum | solution.py:96
  124.7 9.3 %fusion.2 = f32[512,512]{1,0:T(8,128)} fusion(bf16[1792,512]{1,0:T(8,128)(2,1)} %all-reduce.4.cloned.1.call-done), kind=kOutput, calls=%fused_computation.10 | convolution fusion | flops 5638979584 | bytes 2883584 | tf_op jit(solution)/shard_map/dot_general | solution.py:97
  134.0 0.0 all-reduce.6.cloned.1.call-update
  134.0 0.2 all-reduce.8.cloned.1.call-start
  134.2 52.4 %all-reduce.6.cloned.1.call-done.refs_0_ = f32[512,512]{1,0:T(8,128)} async-done(((f32[512,512]{1,0:T(8,128)}), f32[512,512]{1,0:T(8,128)}) %all-reduce.6.cloned.1.call-update) | async-done | bytes 1048592 | tf_op jit(solution)/shard_map/psum | solution.py:97
  186.7 37.8 %inverse_factor.1 = f32[512,512]{1,0:T(8,128)} custom-call(f32[512,512]{1,0:T(8,128)} %all-reduce.6.cloned.1.call-done.refs_0_), custom_call_target="tpu_custom_call" | custom-call | tf_op jit(solution)/shard_map/inverse_factor/pallas_call | solution.py:73
  224.4 7.9 %fusion.3 = bf16[1792,512]{1,0:T(8,128)(2,1)S(1)} fusion(f32[512,512]{1,0:T(8,128)} %inverse_factor.1, bf16[1792,512]{1,0:T(8,128)(2,1)} %all-reduce.4.cloned.1.call-done), kind=kOutput, calls=%fused_computation.11 | convolution fusion | flops 5639897088 | bytes 4718592 | tf_op jit(solution)/shard_map/dot_general | solution.py:99
  232.4 14.4 %fusion.11 = f32[2048,512]{1,0:T(8,128)} fusion(bf16[1792,512]{1,0:T(8,128)(2,1)S(1)} %fusion.3, f32[1,1792,2048]{2,1,0:T(8,128)} %param.5, bf16[1,1792,2048]{2,1,0:T(8,128)(2,1)} %param.6), kind=kOutput, calls=%fused_computation.22 | convolution fusion | flops 3769106432 | bytes 28049408 | tf_op jit(solution)/shard_map/ij,ik->jk/dot_general | solution.py:101
  246.8 0.0 all-reduce.8.cloned.1.call-update
  246.8 142.4 %all-reduce.8.cloned.1.call-done = f32[2048,512]{1,0:T(8,128)} async-done(((f32[2048,512]{1,0:T(8,128)}), f32[2048,512]{1,0:T(8,128)}) %all-reduce.8.cloned.1.call-update) | async-done | bytes 4194320 | tf_op jit(solution)/shard_map/psum | solution.py:104
  389.3 0.0 copy-start
  389.3 2.9 multiply_reduce_fusion
  392.2 0.6 copy-done
  392.7 0.5 multiply_divide_fusion
  393.3 1.0 constant_dynamic-slice_fusion
  394.3 8.2 %subtract_convert_fusion = bf16[1792,2048]{1,0:T(8,128)(2,1)} fusion(bf16[1792,2048]{1,0:T(8,128)(2,1)} %param.4, bf16[1792,512]{1,0:T(8,128)(2,1)S(1)} %fusion.3, f32[2048,512]{1,0:T(8,128)S(1)} %multiply_divide_fusion), kind=kOutput, calls=%fused_computation.3 | convolution fusion | flops 3773825024 | bytes 20709376 | tf_op jit(solution)/shard_map/dot_general | solution.py:109
  402.6 12.6 %fusion = f32[1,1792,2048]{2,1,0:T(8,128)} fusion(f32[1,1792,2048]{2,1,0:T(8,128)} %param.5, bf16[1,1792,2048]{2,1,0:T(8,128)(2,1)} %param.6, bf16[1792,512]{1,0:T(8,128)(2,1)S(1)} %fusion.3, f32[2048,512]{1,0:T(8,128)S(1)} %copy-done), kind=kOutput, calls=%fused_computation.2 | convolution fusion | flops 3774873600 | bytes 42729472 | tf_op jit(solution)/shard_map/dot_general | solution.py:106
  (1 shorter events, 0.0 us)
Async XLA Ops:
  7.2 41.2 %all-gather.2.cloned.1.call-start = ((), (), s32[]{:S(2)}) async-start(), calls=%async_computation | async-start | bytes 2621440 | tf_op jit(solution)/shard_map/all_gather | solution.py:92
  9.3 115.4 %all-reduce.4.cloned.1.call-start = ((), (), s32[]{:S(2)}) async-start(), calls=%async_computation.1 | async-start | bytes 3670016 | tf_op jit(solution)/shard_map/psum | solution.py:96
  61.4 125.2 %all-reduce.6.cloned.1.call-start = ((), (), s32[]{:S(2)}) async-start(), calls=%async_computation.2 | async-start | bytes 2097152 | tf_op jit(solution)/shard_map/psum | solution.py:97
  134.0 255.3 %all-reduce.8.cloned.1.call-start = ((), (), s32[]{:S(2)}) async-start(), calls=%async_computation.3 | async-start | bytes 8388608 | tf_op jit(solution)/shard_map/psum | solution.py:104
  389.3 3.4 copy-start
Sparse Core Ops, SparseCore 0:
  10.4 37.8 all-gather.1
  61.5 63.1 all-reduce.3
  134.1 52.4 all-reduce.5
  247.0 142.2 all-reduce.7

commit v2 on v1

--- a/solution.py
+++ b/solution.py
@@ -1,3 +1,5 @@
+import functools
+
 import jax, jax.numpy as jnp
 from jax import lax
 from jax.experimental import pallas as pl
@@ -80,38 +82,365 @@
     )(gram)
 
 
+MESH = pl.DeviceIdType.MESH
+BF16 = jnp.bfloat16
+
+
+class Net:
+    def __init__(self, parts, shards):
+        self.P, self.R, self.Z = parts, shards, parts // 2
+        self.r, self.j = lax.axis_index("rep"), lax.axis_index("rows")
+        self.z, self.c = self.r // 2, lax.rem(self.r, 2)
+        self.other = 1 - self.c
+        self.partner = (2 * self.z + self.other, self.j)
+
+    def row(self, step):
+        return lax.rem(self.j + step + self.R, self.R)
+
+    def level(self, step):
+        return lax.rem(self.z + step + self.Z, self.Z)
+
+    def row_peer(self, step):
+        return (self.r, self.row(step))
+
+    def level_peer(self, step):
+        return (2 * self.level(step) + self.c, self.j)
+
+    def peers(self):
+        found = [self.partner]
+        found += [self.row_peer(d) for d in range(1, self.R)]
+        found += [self.level_peer(e) for e in range(1, self.Z)]
+        return found
+
+    def greet(self):
+        barrier = pltpu.get_barrier_semaphore()
+        for peer in self.peers():
+            pl.semaphore_signal(barrier, inc=1, device_id=peer, device_id_type=MESH)
+
+    def meet(self):
+        pl.semaphore_wait(pltpu.get_barrier_semaphore(), len(self.peers()))
+
+
+class Lane:
+    def __init__(self, send, recv):
+        self.send, self.recv, self.open = send, recv, []
+
+    def make(self, at, source, target, device):
+        return pltpu.make_async_remote_copy(
+            src_ref=source, dst_ref=target, send_sem=self.send.at[at], recv_sem=self.recv.at[at],
+            device_id=device, device_id_type=MESH,
+        )
+
+    def start(self, at, source, target, device):
+        copy = self.make(at, source, target, device)
+        copy.start()
+        self.open.append(copy)
+
+    def arrive(self, at, target, device):
+        self.make(at, target, target, device).wait_recv()
+
+    def close(self):
+        for copy in self.open:
+            copy.wait_send()
+
+
+def reduce_count(shards, levels):
+    return 4 * shards + 2 * levels
+
+
+def reduce_scratch(parts, shards, piece, width, kind):
+    levels = parts // 2
+    block = (levels, piece, width)
+    return [
+        pltpu.VMEM((2 * shards * levels, piece, width), kind),
+        pltpu.VMEM((2 * shards * levels, piece, width), kind),
+        pltpu.VMEM((shards,) + block, kind),
+        pltpu.VMEM((shards,) + block, kind),
+        pltpu.VMEM((shards,) + block, kind),
+        pltpu.VMEM(block, F32),
+        pltpu.VMEM(block, kind),
+        pltpu.VMEM(block, kind),
+        pltpu.SemaphoreType.DMA((reduce_count(shards, levels),)),
+        pltpu.SemaphoreType.DMA((reduce_count(shards, levels),)),
+    ]
+
+
+def reduce_all(net, scratch, scale):
+    src, out, pair, near, half, acc, quarter, far, send, recv = scratch
+    R, Z, kind = net.R, net.Z, out.dtype
+    lane = Lane(send, recv)
+    a, b, e, f, c, d = 0, R, 2 * R, 3 * R, 4 * R, 4 * R + Z
+
+    def block(core, row):
+        return pl.ds((core * R + row) * Z, Z)
+
+    order = list(range(1, R)) + [0]
+    for s in order:
+        lane.start(a + s, src.at[block(net.other, net.row(s))], pair.at[s], net.partner)
+    for s in order:
+        lane.arrive(a + s, pair.at[s], net.partner)
+        total = src[block(net.c, net.row(s))].astype(F32) + pair[s].astype(F32)
+        if s == 0:
+            acc[...] = total
+        else:
+            half[s] = total.astype(kind)
+            lane.start(b + s, half.at[s], near.at[s], net.row_peer(s))
+    for s in range(1, R):
+        lane.arrive(b + s, near.at[s], net.row_peer(-s))
+        acc[...] = acc[...] + near[s].astype(F32)
+    quarter[...] = acc[...].astype(kind)
+    for s in range(1, Z):
+        lane.start(c + s, quarter.at[net.level(s)], far.at[s], net.level_peer(s))
+    total = acc[net.z]
+    for s in range(1, Z):
+        lane.arrive(c + s, far.at[s], net.level_peer(-s))
+        total = total + far[s].astype(F32)
+    base = (net.c * R + net.j) * Z
+    out[base + net.z] = (total * scale).astype(kind)
+    mine = out.at[base + net.z]
+    for s in range(1, Z):
+        lane.start(d + s, mine, mine, net.level_peer(s))
+    for s in range(1, Z):
+        lane.arrive(d + s, out.at[base + net.level(-s)], net.level_peer(-s))
+    whole = out.at[block(net.c, net.j)]
+    for s in range(1, R):
+        lane.start(e + s, whole, whole, net.row_peer(s))
+    lane.start(f, whole, whole, net.partner)
+    for s in range(1, R):
+        came = out.at[block(net.c, net.row(-s))]
+        lane.arrive(e + s, came, net.row_peer(-s))
+        lane.start(f + s, came, came, net.partner)
+    for s in range(R):
+        lane.arrive(f + s, out.at[block(net.other, net.row(-s))], net.partner)
+    lane.close()
+
+
+def front_kernel(parts, shards, momentum, gradient, right, kept, mean_out, gram_out,
+                 mom, grad, comb, gathered, left, pair, half, far, mean, mom_sem, grad_sem, keep_sem,
+                 out_sem, send, recv, *scratch):
+    net = Net(parts, shards)
+    P, R, Z = net.P, net.R, net.Z
+    for p in range(P):
+        pltpu.make_async_copy(momentum.at[p], mom.at[p], mom_sem.at[p]).start()
+        pltpu.make_async_copy(gradient.at[p], grad.at[p], grad_sem.at[p]).start()
+    net.greet()
+    net.meet()
+    lane = Lane(send, recv)
+    a, b, c, d = 0, R, 2 * R, 2 * R + Z
+    for s in range(1, R):
+        lane.start(a + s, right.at[net.c], gathered.at[net.j, net.c], net.row_peer(s))
+    gathered[net.j] = right[...]
+
+    def combine(p, carry):
+        pltpu.make_async_copy(momentum.at[p], mom.at[p], mom_sem.at[p]).wait()
+        pltpu.make_async_copy(gradient.at[p], grad.at[p], grad_sem.at[p]).wait()
+        comb[p] = (mom[p] + grad[p].astype(F32)).astype(BF16)
+        pltpu.make_async_copy(comb.at[p], kept.at[p], keep_sem.at[p]).start()
+        return carry
+
+    lax.fori_loop(0, P, combine, 0)
+    for s in range(1, R):
+        came = gathered.at[net.row(-s), net.c]
+        lane.arrive(a + s, came, net.row_peer(-s))
+        lane.start(b + s, came, came, net.partner)
+    for s in range(1, R):
+        lane.arrive(b + s, gathered.at[net.row(-s), net.other], net.partner)
+
+    def project(p):
+        full = gathered[...].reshape(comb.shape[2], right.shape[2])
+        left[p] = jnp.dot(comb[p], full, preferred_element_type=F32).astype(BF16)
+
+    def hand_on(s):
+        level = net.level(s)
+        lane.arrive(c + s % Z, pair.at[s % Z], net.partner)
+        if s < Z:
+            half[s] = (left[2 * level + net.c].astype(F32) + pair[s].astype(F32)).astype(BF16)
+            lane.start(d + s, half.at[s], far.at[s], net.level_peer(s))
+
+    for s in range(1, Z + 1):
+        level = net.level(s)
+        project(2 * level + net.other)
+        lane.start(c + s % Z, left.at[2 * level + net.other], pair.at[s % Z], net.partner)
+        project(2 * level + net.c)
+        if s > 1:
+            hand_on(s - 1)
+    hand_on(Z)
+    total = left[net.r].astype(F32) + pair[0].astype(F32)
+    for s in range(1, Z):
+        lane.arrive(d + s, far.at[s], net.level_peer(-s))
+        total = total + far[s].astype(F32)
+    mean[...] = total / P
+    keep_mean = pltpu.make_async_copy(mean, mean_out, out_sem.at[0])
+    keep_mean.start()
+    gram = dot_tn(mean[...], mean[...])
+    src = scratch[0]
+    pieces, piece, _ = src.shape
+    for i in range(pieces):
+        src[i] = gram[i * piece:(i + 1) * piece, :]
+    reduce_all(net, scratch, 1.0)
+    keep_gram = pltpu.make_async_copy(scratch[1], gram_out, out_sem.at[1])
+    keep_gram.start()
+    keep_mean.wait()
+    keep_gram.wait()
+    lane.close()
+    for p in range(P):
+        pltpu.make_async_copy(comb.at[p], kept.at[p], keep_sem.at[p]).wait()
+
+
+def front(momentum, gradient, right):
+    parts, shards = lax.axis_size("rep"), lax.axis_size("rows")
+    levels = parts // 2
+    _, rows, cols = momentum.shape
+    rows = rows // parts
+    depth, width = right.shape
+    piece = width // (shards * parts)
+    anywhere = pl.BlockSpec(memory_space=pl.ANY)
+    inside = pl.BlockSpec(memory_space=pltpu.VMEM)
+    count = 2 * shards + 2 * levels
+    return pl.pallas_call(
+        functools.partial(front_kernel, parts, shards),
+        out_shape=[
+            jax.ShapeDtypeStruct((parts, rows, cols), BF16),
+            jax.ShapeDtypeStruct((rows, width), F32),
+            jax.ShapeDtypeStruct((shards * parts, piece, width), F32),
+        ],
+        in_specs=[anywhere, anywhere, inside],
+        out_specs=[anywhere, anywhere, anywhere],
+        scratch_shapes=[
+            pltpu.VMEM((parts, rows, cols), F32),
+            pltpu.VMEM((parts, rows, cols), BF16),
+            pltpu.VMEM((parts, rows, cols), BF16),
+            pltpu.VMEM((shards, 2, depth // 2, width), BF16),
+            pltpu.VMEM((parts, rows, width), BF16),
+            pltpu.VMEM((levels, rows, width), BF16),
+            pltpu.VMEM((levels, rows, width), BF16),
+            pltpu.VMEM((levels, rows, width), BF16),
+            pltpu.VMEM((rows, width), F32),
+            pltpu.SemaphoreType.DMA((parts,)),
+            pltpu.SemaphoreType.DMA((parts,)),
+            pltpu.SemaphoreType.DMA((parts,)),
+            pltpu.SemaphoreType.DMA((2,)),
+            pltpu.SemaphoreType.DMA((count,)),
+            pltpu.SemaphoreType.DMA((count,)),
+        ] + reduce_scratch(parts, shards, piece, width, F32),
+        compiler_params=pltpu.CompilerParams(collective_id=1, has_side_effects=True, vmem_limit_bytes=60 * 1024 * 1024),
+        name="front",
+    )(
+        momentum.reshape(parts, rows, cols),
+        gradient.reshape(parts, rows, cols),
+        right.reshape(2, depth // 2, width),
+    )
+
+
+def back_kernel(parts, shards, tile, mean, inverse, kept, left_out, right_out,
+                comb, left, partial, comb_sem, out_sem, send, recv, *scratch):
+    net = Net(parts, shards)
+    P, R, Z = net.P, net.R, net.Z
+    net.greet()
+    for p in range(P):
+        pltpu.make_async_copy(kept.at[p], comb.at[p], comb_sem.at[p]).start()
+    own = lax.dot_general(
+        mean[...], inverse[...], (((1,), (1,)), ((), ())), precision=HI, preferred_element_type=F32
+    )
+    left[net.r] = own.astype(BF16)
+    for p in range(P):
+        pltpu.make_async_copy(kept.at[p], comb.at[p], comb_sem.at[p]).wait()
+    net.meet()
+    lane = Lane(send, recv)
+    a, b = 0, Z
+    mine = left.at[net.r]
+    for s in range(1, Z):
+        lane.start(a + s, mine, mine, net.level_peer(s))
+    lane.start(b, mine, mine, net.partner)
+    src = scratch[0]
+    piece = src.shape[1]
+
+    def absorb(s):
+        level = net.level(-s)
+        lane.arrive(b + s, left.at[2 * level + net.other], net.partner)
+
+        def columns(t, carry):
+            at = pl.ds(pl.multiple_of(t * tile, tile), tile)
+            total = None
+            for core in range(2):
+                term = lax.dot_general(
+                    comb[2 * level + core, :, at], left[2 * level + core],
+                    (((0,), (0,)), ((), ())), preferred_element_type=F32,
+                )
+                total = term if total is None else total + term
+            if s > 0:
+                total = total + partial[at, :]
+            if s < Z - 1:
+                partial[at, :] = total
+            else:
+                here = pl.ds(t * (tile // piece), tile // piece)
+                src[here] = total.reshape(tile // piece, piece, total.shape[1]).astype(BF16)
+            return carry
+
+        lax.fori_loop(0, partial.shape[0] // tile, columns, 0)
+
+    for s in range(1, Z):
+        came = left.at[2 * net.level(-s) + net.c]
+        lane.arrive(a + s, came, net.level_peer(-s))
+        lane.start(b + s, came, came, net.partner)
+        absorb(s - 1)
+    absorb(Z - 1)
+    keep_left = pltpu.make_async_copy(left, left_out, out_sem.at[0])
+    keep_left.start()
+    reduce_all(net, scratch, 1.0 / P)
+    keep_right = pltpu.make_async_copy(scratch[1], right_out, out_sem.at[1])
+    keep_right.start()
+    keep_left.wait()
+    keep_right.wait()
+    lane.close()
+
+
+def back(mean, inverse, kept):
+    parts, shards = lax.axis_size("rep"), lax.axis_size("rows")
+    levels = parts // 2
+    _, rows, cols = kept.shape
+    width = mean.shape[1]
+    piece = cols // (shards * parts)
+    anywhere = pl.BlockSpec(memory_space=pl.ANY)
+    inside = pl.BlockSpec(memory_space=pltpu.VMEM)
+    return pl.pallas_call(
+        functools.partial(back_kernel, parts, shards, 256),
+        out_shape=[
+            jax.ShapeDtypeStruct((parts, rows, width), BF16),
+            jax.ShapeDtypeStruct((shards * parts, piece, width), BF16),
+        ],
+        in_specs=[inside, inside, anywhere],
+        out_specs=[anywhere, anywhere],
+        scratch_shapes=[
+            pltpu.VMEM((parts, rows, cols), BF16),
+            pltpu.VMEM((parts, rows, width), BF16),
+            pltpu.VMEM((cols, width), F32),
+            pltpu.SemaphoreType.DMA((parts,)),
+            pltpu.SemaphoreType.DMA((2,)),
+            pltpu.SemaphoreType.DMA((2 * levels,)),
+            pltpu.SemaphoreType.DMA((2 * levels,)),
+        ] + reduce_scratch(parts, shards, piece, width, BF16),
+        compiler_params=pltpu.CompilerParams(collective_id=2, has_side_effects=True, vmem_limit_bytes=60 * 1024 * 1024),
+        name="back",
+    )(mean, inverse, kept)
+
+
 def per_device(weights, momentum, gradient, right_factor):
-    groups = lax.axis_size("rep")
     shards = lax.axis_size("rows")
-    combined = momentum[0] + gradient[0].astype(jnp.float32)
-    combined_half = combined.astype(jnp.bfloat16)
-    columns = combined.shape[1]
-    share = columns // shards
-    left_local = jnp.dot(
-        combined_half,
-        lax.all_gather(right_factor.astype(jnp.bfloat16), "rows", axis=0, tiled=True),
-        preferred_element_type=jnp.float32,
-    )
-    left_local = lax.optimization_barrier(left_local.astype(jnp.bfloat16)).astype(jnp.float32)
-    left_mean = lax.psum(left_local.astype(jnp.bfloat16), "rep").astype(jnp.float32) / groups
-    gram = lax.psum(jnp.dot(left_mean.T, left_mean, precision=lax.Precision.HIGHEST), "rows")
-    inverse = inverse_factor(gram)
-    left_orth = jnp.dot(left_mean, inverse.T, precision=lax.Precision.HIGHEST)
-    left_half = left_orth.astype(jnp.bfloat16)
-    partial_right = jnp.einsum(
-        "ij,ik->jk", combined_half, left_half, preferred_element_type=jnp.float32
-    )
-    right_mean = lax.psum(partial_right, ("rep", "rows")) / groups
+    kept, mean, gram = front(momentum, gradient, right_factor.astype(BF16))
+    width = right_factor.shape[1]
+    inverse = inverse_factor(gram.reshape(width, width))
+    left_parts, right_parts = back(mean, inverse, kept)
+    left_half = left_parts.reshape(weights.shape[0], width)
+    right_half = right_parts.reshape(weights.shape[1], width)
+    right_mean = right_half.astype(F32)
     normed = right_mean / jnp.sqrt(jnp.mean(right_mean * right_mean, axis=0) + tiny)
-    feedback = jnp.dot(
-        left_half, right_mean.astype(jnp.bfloat16).T, preferred_element_type=jnp.float32
-    )
-    update = jnp.dot(left_half, normed.astype(jnp.bfloat16).T, preferred_element_type=jnp.float32)
+    feedback = jnp.dot(left_half, right_half.T, preferred_element_type=F32)
+    update = jnp.dot(left_half, normed.astype(BF16).T, preferred_element_type=F32)
+    share = weights.shape[1] // shards
     new_right = lax.dynamic_slice_in_dim(normed, lax.axis_index("rows") * share, share, 0)
-    new_momentum = combined - momentum_keep * feedback
-    new_weights = (weights.astype(jnp.float32) - learn_rate * jnp.sqrt(M / N) * update).astype(
-        jnp.bfloat16
-    )
+    new_momentum = momentum[0] + gradient[0].astype(F32) - momentum_keep * feedback
+    new_weights = (weights.astype(F32) - learn_rate * jnp.sqrt(M / N) * update).astype(BF16)
     return (new_weights, new_momentum[None], new_right)
 
 

time: 430 us -> 217 us (0.50); the launches traced: 422 us -> 217 us
  waiting for transfers between devices: 297 us -> 0 us
  Pallas kernels: 37.8 us -> 188 us
  matrix products: 65.6 us -> 19.8 us
  between operations: 14.2 us -> 0.71 us
    psum x3 -> x0, waiting for transfers between devices: 258 us -> none  [the longest x1 142 us: per_device(): right_mean = lax.psum(partial_right, ('rep', 'rows')) / groups]
    pallas_call x0 -> x2, Pallas kernels: none -> 151 us  [the longest x1 78.2 us: back(): pl.pallas_call(functools.partial(back_kernel, parts, shards, 256), out_sh...]
    dot_general x6 -> x2, matrix products: 65.6 us -> 19.8 us  [the longest x1 11.3 us: per_device(): feedback = jnp.dot(left_half, right_half.T, preferred_element_type=F32)]
    all_gather x1 -> x0, waiting for transfers between devices: 39 us -> none  [per_device(): lax.all_gather(right_factor.astype(jnp.bfloat16), 'rows', axis=0, tiled=T...]
  transfers between devices with their start and end apart: 4 -> 0, of which waited for: 4 -> 0; matrix products, arithmetic and copies ran while one was open for 0% -> 0% of each run, Pallas kernels for 0% -> 0%
where the time goes in v2:
time: 217 us
  Pallas kernels  188 us (87%)
  matrix products  19.8 us (9%)
  other arithmetic  7.76 us (4%)
    pallas_call x1, Pallas kernels, back(): pl.pallas_call(functools.partial(back_kernel, parts, shards, 256), out_sh...  78.2 us
    pallas_call x1, Pallas kernels, front(): pl.pallas_call(functools.partial(front_kernel, parts, shards), out_shape=...  72.3 us
    pallas_call x1, Pallas kernels, inverse_factor(): pl.pallas_call(lambda *refs: chol_kernel(size, 8, *refs), out_shape=jax.S...  37.9 us
    dot_general x1, matrix products, per_device(): feedback = jnp.dot(left_half, right_half.T, preferred_element_type=F32)  11.3 us
    dot_general x1, matrix products, per_device(): jnp.dot(left_half, normed.astype(BF16).T, preferred_element_type=F32)  8.49 us

profile of v2, /device:TPU:0, one launch (start us, length us, event | category | flops | bytes accessed | tf_op | source)
XLA Modules:
  0.0 216.8 jit_solution(741167183951903392)
XLA Ops:
  0.6 2.1 convert_element_type.27
  2.7 72.3 %front.1 = (bf16[8,224,2048]{2,1,0:T(8,128)(2,1)}, f32[224,512]{1,0:T(8,128)}, f32[32,16,512]{2,1,0:T(8,128)}) custom-call(f32[8,224,2048]{2,1,0:T(8,128)} %bitcast.17, bf16[8,224,2048]{2,1,0:T(8,128)(2,1)} %bitcast.20, bf16[2,256,512]{2,1,0:T(8,128)(2,1)} %bitcast.23), custom_call_target="tpu_custom_call" | custom-call | tf_op jit(solution)/shard_map/front/pallas_call | solution.py:300
  75.0 37.9 %inverse_factor.1.inverse = f32[512,512]{1,0:T(8,128)} custom-call(f32[512,512]{1,0:T(8,128)} %bitcast.25), custom_call_target="tpu_custom_call" | custom-call | tf_op jit(solution)/shard_map/inverse_factor/pallas_call | solution.py:75
  113.0 78.2 %back.1 = (bf16[8,224,512]{2,1,0:T(8,128)(2,1)}, bf16[32,64,512]{2,1,0:T(8,128)(2,1)}) custom-call(f32[224,512]{1,0:T(8,128)} %get-tuple-element.8.mean, f32[512,512]{1,0:T(8,128)} %inverse_factor.1.inverse, bf16[8,224,2048]{2,1,0:T(8,128)(2,1)} %get-tuple-element.10.kept), custom_call_target="tpu_custom_call" | custom-call | tf_op jit(solution)/shard_map/back/pallas_call | solution.py:406
  191.2 0.0 copy-start.1
  191.2 2.3 %fusion.1 = f32[512]{0:T(512)S(1)} fusion(bf16[32,64,512]{2,1,0:T(8,128)(2,1)} %get-tuple-element.12), kind=kLoop, calls=%fused_computation.5 | loop fusion | flops 3145216 | bytes 2099200 | tf_op jit(solution)/shard_map/reduce_sum | solution.py:437
  193.5 0.0 slice-start
  193.5 2.3 %fusion.2 = bf16[32,64,512]{2,1,0:T(8,128)(2,1)S(1)} fusion(bf16[32,64,512]{2,1,0:T(8,128)(2,1)} %get-tuple-element.12, f32[512]{0:T(512)S(1)} %add_sqrt_fusion), kind=kLoop, calls=%fused_computation.6 | loop fusion | flops 3145728 | bytes 4196352 | tf_op jit(solution)/shard_map/convert_element_type | solution.py:439
  195.8 0.0 copy-done.1
  195.8 0.0 copy-start
  195.8 0.0 slice-start.1
  195.8 8.5 %subtract_convert_fusion = bf16[1792,2048]{1,0:T(8,128)(2,1)} fusion(bf16[1792,2048]{1,0:T(8,128)(2,1)} %param.4, bf16[1792,512]{1,0:T(8,128)(2,1)S(1)} %bitcast.27, bf16[2048,512]{1,0:T(8,128)(2,1)S(1)} %bitcast.24), kind=kOutput, calls=%fused_computation.2 | convolution fusion | flops 3772776448 | bytes 18612224 | tf_op jit(solution)/shard_map/dot_general | solution.py:439
  204.3 0.0 slice-done
  204.3 0.0 copy-done
  204.3 0.0 slice-done.1
  204.3 11.3 %fusion = f32[1,1792,2048]{2,1,0:T(8,128)} fusion(f32[1,1792,2048]{2,1,0:T(8,128)} %param.5, bf16[1,1792,2048]{2,1,0:T(8,128)(2,1)S(1)} %bitcast.22, bf16[1792,512]{1,0:T(8,128)(2,1)} %bitcast.26, bf16[2048,512]{1,0:T(8,128)(2,1)S(1)} %bitcast.18), kind=kOutput, calls=%fused_computation.1 | convolution fusion | flops 3772776448 | bytes 40632320 | tf_op jit(solution)/shard_map/dot_general | solution.py:438
  215.6 1.1 convert_divide_fusion.1
  (2 shorter events, 0.0 us)
Async XLA Ops:
  191.2 4.6 %copy-start.1 = (bf16[8,224,512]{2,1,0:T(8,128)(2,1)S(1)}, bf16[8,224,512]{2,1,0:T(8,128)(2,1)}, u32[]{:S(2)}) copy-start(bf16[8,224,512]{2,1,0:T(8,128)(2,1)} %get-tuple-element.11) | copy-start | bytes 5505028
  193.5 10.8 %slice-start = ((s8[7340032]{0:T(1024)(128)(4,1)}), s8[4194304]{0:T(1024)(128)(4,1)S(1)}, s32[]{:S(2)}) async-start(s8[7340032]{0:T(1024)(128)(4,1)} %bitcast.21), calls=%async_computation | async-start | bytes 8388608
  195.8 8.5 %copy-start = (bf16[32,64,512]{2,1,0:T(8,128)(2,1)S(1)}, bf16[32,64,512]{2,1,0:T(8,128)(2,1)}, u32[]{:S(2)}) copy-start(bf16[32,64,512]{2,1,0:T(8,128)(2,1)} %get-tuple-element.12) | copy-start | bytes 6291460
  195.8 8.5 %slice-start.1 = ((s8[7340032]{0:T(1024)(128)(4,1)}), s8[3145728]{0:T(1024)(128)(4,1)S(1)}, s32[]{:S(2)}) async-start(s8[7340032]{0:T(1024)(128)(4,1)} %bitcast.21), calls=%async_computation.1 | async-start | bytes 6291456

commit v3 on v2

--- a/solution.py
+++ b/solution.py
@@ -1,4 +1,5 @@
 import functools
+import math
 
 import jax, jax.numpy as jnp
 from jax import lax
@@ -50,8 +51,12 @@
             work[nxt:, :] = work[nxt:, :] - upd[nxt:, :]
 
 def chol_kernel(size, step, gram_ref, out_ref, full, work):
-    rank = gram_ref.shape[0]
-    full[:, :rank] = gram_ref[...]
+    rank = full.shape[0]
+    stacks, slots = packing(rank)
+    full[:, :rank] = jnp.zeros((rank, rank), F32)
+    for (i, k), (stack, at) in slots.items():
+        block = gram_ref[stack * BLOCK:(stack + 1) * BLOCK, at:at + BLOCK]
+        full[i * BLOCK:(i + 1) * BLOCK, k * BLOCK:(k + 1) * BLOCK] = block
     r = lax.broadcasted_iota(jnp.int32, (rank, rank), 0)
     c = lax.broadcasted_iota(jnp.int32, (rank, rank), 1)
     full[:, rank:] = jnp.where(r == c, 1.0, 0.0).astype(F32)
@@ -69,11 +74,10 @@
         if nxt < rank:
             full[nxt:, :] = full[nxt:, :] - dot_tn(block[:, nxt:rank], block)
 
-def inverse_factor(gram):
-    rank = gram.shape[0]
-    size = 128
+def inverse_factor(gram, rank):
+    size = BLOCK
     return pl.pallas_call(
-        lambda *refs: chol_kernel(size, 8, *refs),
+        lambda *refs: chol_kernel(size, 16, *refs),
         out_shape=jax.ShapeDtypeStruct((rank, rank), F32),
         in_specs=[pl.BlockSpec(memory_space=pltpu.VMEM)],
         out_specs=pl.BlockSpec(memory_space=pltpu.VMEM),
@@ -215,6 +219,22 @@
     lane.close()
 
 
+BLOCK = 128
+
+
+def packing(width):
+    count = width // BLOCK
+    names = [(i, k) for i in range(count) for k in range(i, count)]
+    stacks = 2 if len(names) % 2 == 0 else 1
+    each = len(names) // stacks
+    return stacks, {name: (n // each, (n % each) * BLOCK) for n, name in enumerate(names)}
+
+
+def packed_shape(width, pieces):
+    stacks, slots = packing(width)
+    return pieces, stacks * BLOCK // pieces, len(slots) // stacks * BLOCK
+
+
 def front_kernel(parts, shards, momentum, gradient, right, kept, mean_out, gram_out,
                  mom, grad, comb, gathered, left, pair, half, far, mean, mom_sem, grad_sem, keep_sem,
                  out_sem, send, recv, *scratch):
@@ -272,11 +292,17 @@
     mean[...] = total / P
     keep_mean = pltpu.make_async_copy(mean, mean_out, out_sem.at[0])
     keep_mean.start()
-    gram = dot_tn(mean[...], mean[...])
     src = scratch[0]
     pieces, piece, _ = src.shape
-    for i in range(pieces):
-        src[i] = gram[i * piece:(i + 1) * piece, :]
+    stacks, slots = packing(mean.shape[1])
+    spread = BLOCK // (pieces // stacks)
+    for i in range(mean.shape[1] // BLOCK):
+        gram = dot_tn(mean[:, i * BLOCK:(i + 1) * BLOCK], mean[:, i * BLOCK:])
+        for k in range(i, mean.shape[1] // BLOCK):
+            stack, at = slots[i, k]
+            block = gram[:, (k - i) * BLOCK:(k - i + 1) * BLOCK]
+            for m in range(pieces // stacks):
+                src[stack * (pieces // stacks) + m, :, at:at + BLOCK] = block[m * spread:(m + 1) * spread, :]
     reduce_all(net, scratch, 1.0)
     keep_gram = pltpu.make_async_copy(scratch[1], gram_out, out_sem.at[1])
     keep_gram.start()
@@ -293,7 +319,7 @@
     _, rows, cols = momentum.shape
     rows = rows // parts
     depth, width = right.shape
-    piece = width // (shards * parts)
+    packed = packed_shape(width, shards * parts)
     anywhere = pl.BlockSpec(memory_space=pl.ANY)
     inside = pl.BlockSpec(memory_space=pltpu.VMEM)
     count = 2 * shards + 2 * levels
@@ -302,7 +328,7 @@
         out_shape=[
             jax.ShapeDtypeStruct((parts, rows, cols), BF16),
             jax.ShapeDtypeStruct((rows, width), F32),
-            jax.ShapeDtypeStruct((shards * parts, piece, width), F32),
+            jax.ShapeDtypeStruct(packed, F32),
         ],
         in_specs=[anywhere, anywhere, inside],
         out_specs=[anywhere, anywhere, anywhere],
@@ -322,7 +348,7 @@
             pltpu.SemaphoreType.DMA((2,)),
             pltpu.SemaphoreType.DMA((count,)),
             pltpu.SemaphoreType.DMA((count,)),
-        ] + reduce_scratch(parts, shards, piece, width, F32),
+        ] + reduce_scratch(parts, shards, packed[1], packed[2], F32),
         compiler_params=pltpu.CompilerParams(collective_id=1, has_side_effects=True, vmem_limit_bytes=60 * 1024 * 1024),
         name="front",
     )(
@@ -425,22 +451,61 @@
     )(mean, inverse, kept)
 
 
+def final_kernel(scale, left, right, weights, momentum, gradient, weights_out, momentum_out, right_out, normed):
+    share = right_out.shape[0]
+
+    @pl.when(pl.program_id(0) == 0)
+    def _():
+        mean = right[...].astype(F32)
+        length = jnp.sqrt(jnp.mean(mean * mean, axis=0, keepdims=True) + tiny)
+        normed[...] = (mean / length).astype(BF16)
+        at = pl.ds(pl.multiple_of(lax.axis_index("rows") * share, share), share)
+        right_out[...] = right[at, :].astype(F32) / length
+
+    nt = (((1,), (1,)), ((), ()))
+    feedback = lax.dot_general(left[...], right[...], nt, preferred_element_type=F32)
+    momentum_out[...] = momentum[...] + gradient[...].astype(F32) - momentum_keep * feedback
+    update = lax.dot_general(left[...], normed[...], nt, preferred_element_type=F32)
+    weights_out[...] = (weights[...].astype(F32) - scale * update).astype(BF16)
+
+
+def final(left, right, weights, momentum, gradient):
+    rows, cols = weights.shape
+    width = right.shape[1]
+    share = cols // lax.axis_size("rows")
+    tile = next(t for t in (256, 224, 128, 64, 32, 16, 8) if rows % t == 0)
+    scale = learn_rate * math.sqrt(M / N)
+
+    def streamed(columns):
+        return pl.BlockSpec((tile, columns), lambda i: (i, 0))
+
+    def fixed(shape):
+        return pl.BlockSpec(shape, lambda i: (0, 0))
+
+    return pl.pallas_call(
+        functools.partial(final_kernel, scale),
+        grid=(rows // tile,),
+        out_shape=[
+            jax.ShapeDtypeStruct((rows, cols), BF16),
+            jax.ShapeDtypeStruct((rows, cols), F32),
+            jax.ShapeDtypeStruct((share, width), F32),
+        ],
+        in_specs=[streamed(width), fixed((cols, width)), streamed(cols), streamed(cols), streamed(cols)],
+        out_specs=[streamed(cols), streamed(cols), fixed((share, width))],
+        scratch_shapes=[pltpu.VMEM((cols, width), BF16)],
+        compiler_params=pltpu.CompilerParams(vmem_limit_bytes=60 * 1024 * 1024),
+        name="final",
+    )(left, right, weights, momentum, gradient)
+
+
 def per_device(weights, momentum, gradient, right_factor):
-    shards = lax.axis_size("rows")
     kept, mean, gram = front(momentum, gradient, right_factor.astype(BF16))
     width = right_factor.shape[1]
-    inverse = inverse_factor(gram.reshape(width, width))
+    inverse = inverse_factor(gram.reshape(-1, gram.shape[2]), width)
     left_parts, right_parts = back(mean, inverse, kept)
     left_half = left_parts.reshape(weights.shape[0], width)
     right_half = right_parts.reshape(weights.shape[1], width)
-    right_mean = right_half.astype(F32)
-    normed = right_mean / jnp.sqrt(jnp.mean(right_mean * right_mean, axis=0) + tiny)
-    feedback = jnp.dot(left_half, right_half.T, preferred_element_type=F32)
-    update = jnp.dot(left_half, normed.astype(BF16).T, preferred_element_type=F32)
-    share = weights.shape[1] // shards
-    new_right = lax.dynamic_slice_in_dim(normed, lax.axis_index("rows") * share, share, 0)
-    new_momentum = momentum[0] + gradient[0].astype(F32) - momentum_keep * feedback
-    new_weights = (weights.astype(F32) - learn_rate * jnp.sqrt(M / N) * update).astype(BF16)
+    new_weights, new_momentum, new_right = final(left_half, right_half, weights, momentum[0], gradient[0])
     return (new_weights, new_momentum[None], new_right)
 
 

time: 217 us -> 204 us (0.940)
  matrix products: 19.8 us -> 0 us
  Pallas kernels: 188 us -> 201 us
  other arithmetic: 7.76 us -> 2.08 us
    dot_general x2 -> x0, matrix products: 19.8 us -> none  [the longest x1 11.3 us: per_device(): feedback = jnp.dot(left_half, right_half.T, preferred_element_type=F32)]
    pallas_call x1 -> x2, Pallas kernels: 37.9 us -> 54.9 us  [the longest x1 30.4 us: inverse_factor(): pl.pallas_call(lambda *refs: chol_kernel(size, 16, *refs), out_shape=jax....]
    pallas_call x1, Pallas kernels: 72.3 us -> 67.9 us  [front(): pl.pallas_call(functools.partial(front_kernel, parts, shards), out_shape=...]
    reduce_sum x1 -> x0, other arithmetic: 2.28 us -> none  [per_device(): jnp.mean(right_mean * right_mean, axis=0) + tiny]
    convert_element_type x1 -> x0, other arithmetic: 2.27 us -> none  [per_device(): normed.astype(BF16)]
where the time goes in v3:
time: 204 us
  Pallas kernels  201 us (99%)
  other arithmetic  2.08 us (1%)
    pallas_call x1, Pallas kernels, back(): pl.pallas_call(functools.partial(back_kernel, parts, shards, 256), out_sh...  78 us
    pallas_call x1, Pallas kernels, front(): pl.pallas_call(functools.partial(front_kernel, parts, shards), out_shape=...  67.9 us
    pallas_call x1, Pallas kernels, inverse_factor(): pl.pallas_call(lambda *refs: chol_kernel(size, 16, *refs), out_shape=jax....  30.4 us
    pallas_call x1, Pallas kernels, final(): pl.pallas_call(functools.partial(final_kernel, scale), grid=(rows // tile...  24.5 us

profile of v3, /device:TPU:0, one launch (start us, length us, event | category | flops | bytes accessed | tf_op | source)
XLA Modules:
  0.0 203.5 jit_solution(6290125721362849103)
XLA Ops:
  0.6 2.1 %convert_element_type.3 = bf16[512,512]{1,0:T(8,128)(2,1)} convert(f32[512,512]{1,0:T(8,128)} %param.7) | non-fusion elementwise | flops 262144 | bytes 1572864 | tf_op jit(solution)/shard_map/convert_element_type | solution.py:502
  2.7 67.9 %front.1 = (bf16[8,224,2048]{2,1,0:T(8,128)(2,1)}, f32[224,512]{1,0:T(8,128)}, f32[32,8,640]{2,1,0:T(8,128)}) custom-call(f32[8,224,2048]{2,1,0:T(8,128)} %bitcast.9, bf16[8,224,2048]{2,1,0:T(8,128)(2,1)} %bitcast.11, bf16[2,256,512]{2,1,0:T(8,128)(2,1)} %bitcast.14), custom_call_target="tpu_custom_call" | custom-call | tf_op jit(solution)/shard_map/front/pallas_call | solution.py:326
  70.6 30.4 %inverse_factor.1.inverse = f32[512,512]{1,0:T(8,128)} custom-call(f32[256,640]{1,0:T(8,128)} %bitcast.16), custom_call_target="tpu_custom_call" | custom-call | tf_op jit(solution)/shard_map/inverse_factor/pallas_call | solution.py:79
  101.0 78.0 %back.1 = (bf16[8,224,512]{2,1,0:T(8,128)(2,1)}, bf16[32,64,512]{2,1,0:T(8,128)(2,1)}) custom-call(f32[224,512]{1,0:T(8,128)} %get-tuple-element.11.mean, f32[512,512]{1,0:T(8,128)} %inverse_factor.1.inverse, bf16[8,224,2048]{2,1,0:T(8,128)(2,1)} %get-tuple-element.13.kept), custom_call_target="tpu_custom_call" | custom-call | tf_op jit(solution)/shard_map/back/pallas_call | solution.py:432
  179.0 24.5 %final.1 = (bf16[1792,2048]{1,0:T(8,128)(2,1)}, f32[1792,2048]{1,0:T(8,128)}, f32[512,512]{1,0:T(8,128)}) custom-call(bf16[1792,512]{1,0:T(8,128)(2,1)} %bitcast.15, bf16[2048,512]{1,0:T(8,128)(2,1)} %bitcast.13, bf16[1792,2048]{1,0:T(8,128)(2,1)} %weights.1, f32[1792,2048]{1,0:T(8,128)} %bitcast.10, bf16[1792,2048]{1,0:T(8,128)(2,1)} %bitcast.12), custom_call_target="tpu_custom_call" | custom-call | tf_op jit(solution)/shard_map/final/pallas_call | solution.py:485

commit v4 on v3

--- a/solution.py
+++ b/solution.py
@@ -21,6 +21,21 @@
 
 def dot_tn(a, b):
     return lax.dot_general(a, b, (((0,), (0,)), ((), ())), precision=HI, preferred_element_type=F32)
+
+def thirds(a):
+    high = a.astype(jnp.bfloat16)
+    rest = a - high.astype(F32)
+    middle = rest.astype(jnp.bfloat16)
+    return high, middle, (rest - middle.astype(F32)).astype(jnp.bfloat16)
+
+
+def dot_thin(a, b):
+    ah, am, al = thirds(a)
+    bh, bm, bl = thirds(b)
+    lhs = jnp.concatenate([ah, ah, am, am, ah, al], axis=0)
+    rhs = jnp.concatenate([bh, bm, bh, bm, bl, bh], axis=0)
+    return lax.dot_general(lhs, rhs, (((0,), (0,)), ((), ())), preferred_element_type=F32)
+
 
 def factor_block(work, size, step):
     wide = 2 * size
@@ -47,7 +62,7 @@
         work[at:at + step, size:] = aug
         nxt = at + step
         if nxt < size:
-            upd = dot_tn(upper, jnp.concatenate([upper, aug], axis=1))
+            upd = dot_thin(upper, jnp.concatenate([upper, aug], axis=1))
             work[nxt:, :] = work[nxt:, :] - upd[nxt:, :]
 
 def chol_kernel(size, step, gram_ref, out_ref, full, work):
@@ -244,12 +259,13 @@
         pltpu.make_async_copy(momentum.at[p], mom.at[p], mom_sem.at[p]).start()
         pltpu.make_async_copy(gradient.at[p], grad.at[p], grad_sem.at[p]).start()
     net.greet()
+    gathered[net.j] = right[...].astype(BF16)
     net.meet()
     lane = Lane(send, recv)
     a, b, c, d = 0, R, 2 * R, 2 * R + Z
     for s in range(1, R):
-        lane.start(a + s, right.at[net.c], gathered.at[net.j, net.c], net.row_peer(s))
-    gathered[net.j] = right[...]
+        own = gathered.at[net.j, net.c]
+        lane.start(a + s, own, own, net.row_peer(s))
 
     def combine(p, carry):
         pltpu.make_async_copy(momentum.at[p], mom.at[p], mom_sem.at[p]).wait()
@@ -369,8 +385,6 @@
         mean[...], inverse[...], (((1,), (1,)), ((), ())), precision=HI, preferred_element_type=F32
     )
     left[net.r] = own.astype(BF16)
-    for p in range(P):
-        pltpu.make_async_copy(kept.at[p], comb.at[p], comb_sem.at[p]).wait()
     net.meet()
     lane = Lane(send, recv)
     a, b = 0, Z
@@ -378,6 +392,8 @@
     for s in range(1, Z):
         lane.start(a + s, mine, mine, net.level_peer(s))
     lane.start(b, mine, mine, net.partner)
+    for p in range(P):
+        pltpu.make_async_copy(kept.at[p], comb.at[p], comb_sem.at[p]).wait()
     src = scratch[0]
     piece = src.shape[1]
 
@@ -451,21 +467,21 @@
     )(mean, inverse, kept)
 
 
-def final_kernel(scale, left, right, weights, momentum, gradient, weights_out, momentum_out, right_out, normed):
+def final_kernel(scale, left, right, weights, momentum, gradient, weights_out, momentum_out, right_out, turned, normed):
     share = right_out.shape[0]
 
     @pl.when(pl.program_id(0) == 0)
     def _():
         mean = right[...].astype(F32)
         length = jnp.sqrt(jnp.mean(mean * mean, axis=0, keepdims=True) + tiny)
-        normed[...] = (mean / length).astype(BF16)
+        turned[...] = right[...].T
+        normed[...] = (mean / length).astype(BF16).T
         at = pl.ds(pl.multiple_of(lax.axis_index("rows") * share, share), share)
         right_out[...] = right[at, :].astype(F32) / length
 
-    nt = (((1,), (1,)), ((), ()))
-    feedback = lax.dot_general(left[...], right[...], nt, preferred_element_type=F32)
+    feedback = jnp.dot(left[...], turned[...], preferred_element_type=F32)
     momentum_out[...] = momentum[...] + gradient[...].astype(F32) - momentum_keep * feedback
-    update = lax.dot_general(left[...], normed[...], nt, preferred_element_type=F32)
+    update = jnp.dot(left[...], normed[...], preferred_element_type=F32)
     weights_out[...] = (weights[...].astype(F32) - scale * update).astype(BF16)
 
 
@@ -492,14 +508,14 @@
         ],
         in_specs=[streamed(width), fixed((cols, width)), streamed(cols), streamed(cols), streamed(cols)],
         out_specs=[streamed(cols), streamed(cols), fixed((share, width))],
-        scratch_shapes=[pltpu.VMEM((cols, width), BF16)],
+        scratch_shapes=[pltpu.VMEM((width, cols), BF16), pltpu.VMEM((width, cols), BF16)],
         compiler_params=pltpu.CompilerParams(vmem_limit_bytes=60 * 1024 * 1024),
         name="final",
     )(left, right, weights, momentum, gradient)
 
 
 def per_device(weights, momentum, gradient, right_factor):
-    kept, mean, gram = front(momentum, gradient, right_factor.astype(BF16))
+    kept, mean, gram = front(momentum, gradient, right_factor)
     width = right_factor.shape[1]
     inverse = inverse_factor(gram.reshape(-1, gram.shape[2]), width)
     left_parts, right_parts = back(mean, inverse, kept)

time: 204 us -> 195 us (0.956)
  Pallas kernels: 201 us -> 194 us
  other arithmetic: 2.08 us -> 0 us
    pallas_call x1, Pallas kernels: 30.4 us -> 25.2 us  [inverse_factor(): pl.pallas_call(lambda *refs: chol_kernel(size, 16, *refs), out_shape=jax....]
    convert_element_type x1 -> x0, other arithmetic: 2.08 us -> none  [per_device(): kept, mean, gram = front(momentum, gradient, right_factor.astype(BF16))]
where the time goes in v4:
time: 195 us
  Pallas kernels  194 us (99%)
    pallas_call x1, Pallas kernels, back(): pl.pallas_call(functools.partial(back_kernel, parts, shards, 256), out_sh...  76.2 us
    pallas_call x1, Pallas kernels, front(): pl.pallas_call(functools.partial(front_kernel, parts, shards), out_shape=...  68.1 us
    pallas_call x1, Pallas kernels, inverse_factor(): pl.pallas_call(lambda *refs: chol_kernel(size, 16, *refs), out_shape=jax....  25.2 us
    pallas_call x1, Pallas kernels, final(): pl.pallas_call(functools.partial(final_kernel, scale), grid=(rows // tile...  24.8 us

profile of v4, /device:TPU:0, one launch (start us, length us, event | category | flops | bytes accessed | tf_op | source)
XLA Modules:
  0.0 195.0 jit_solution(11543781273793316906)
XLA Ops:
  0.6 68.1 %front.1 = (bf16[8,224,2048]{2,1,0:T(8,128)(2,1)}, f32[224,512]{1,0:T(8,128)}, f32[32,8,640]{2,1,0:T(8,128)}) custom-call(f32[8,224,2048]{2,1,0:T(8,128)} %bitcast.9, bf16[8,224,2048]{2,1,0:T(8,128)(2,1)} %bitcast.11, f32[2,256,512]{2,1,0:T(8,128)} %bitcast.15), custom_call_target="tpu_custom_call" | custom-call | tf_op jit(solution)/shard_map/front/pallas_call | solution.py:342
  68.8 25.2 %inverse_factor.1.inverse = f32[512,512]{1,0:T(8,128)} custom-call(f32[256,640]{1,0:T(8,128)} %bitcast.16), custom_call_target="tpu_custom_call" | custom-call | tf_op jit(solution)/shard_map/inverse_factor/pallas_call | solution.py:94
  93.9 76.2 %back.1 = (bf16[8,224,512]{2,1,0:T(8,128)(2,1)}, bf16[32,64,512]{2,1,0:T(8,128)(2,1)}) custom-call(f32[224,512]{1,0:T(8,128)} %get-tuple-element.11.mean, f32[512,512]{1,0:T(8,128)} %inverse_factor.1.inverse, bf16[8,224,2048]{2,1,0:T(8,128)(2,1)} %get-tuple-element.13.kept), custom_call_target="tpu_custom_call" | custom-call | tf_op jit(solution)/shard_map/back/pallas_call | solution.py:448
  170.2 24.8 %final.1 = (bf16[1792,2048]{1,0:T(8,128)(2,1)}, f32[1792,2048]{1,0:T(8,128)}, f32[512,512]{1,0:T(8,128)}) custom-call(bf16[1792,512]{1,0:T(8,128)(2,1)} %bitcast.14, bf16[2048,512]{1,0:T(8,128)(2,1)} %bitcast.13, bf16[1792,2048]{1,0:T(8,128)(2,1)} %weights.1, f32[1792,2048]{1,0:T(8,128)} %bitcast.10, bf16[1792,2048]{1,0:T(8,128)(2,1)} %bitcast.12), custom_call_target="tpu_custom_call" | custom-call | tf_op jit(solution)/shard_map/final/pallas_call | solution.py:501
